TPU v7x, 256 devices: a whole 4x4x8 slice. The times are simulated.
256 devices in a mesh: dom: 32 (over z, y), batch: 8 (over x, core).
Axes of the slice: x: 4, y: 4, z: 8, core: 2. Of those that a mesh axis runs over, the one named last changes fastest.
Arguments:
- activations: bfloat16 [2048, 65536], P('batch', 'dom'), may hold values from 0 to 2
- tile_weights: bfloat16 [4, 512, 512, 128], P(None, 'dom', 'batch'), may hold values from -0.375 to 0.375
- biases: float32 [4, 65536], P(None, 'dom'), may hold values from -2.5 to 2.5
- source_codes: int32 [4, 512, 4], P(None, 'dom'), may hold values from 0 to 19
- send_list: int32 [4, 32, 4], P(None, 'dom'), may hold values from 0 to 15
Outputs:
- result: bfloat16 [2048, 65536], P('batch', 'dom')
All inputs are finite; a program needn't handle non-finite values.
Results may differ from a plain program's by a relative error of at most 0.0062.
Values may be sent and summed in bfloat16 or wider, within the bound.
A program may use at most 64 MiB of HBM per device.

v0:
```python
import jax
import jax.numpy as jnp
from jax import lax
from jax.sharding import PartitionSpec as P


def body(activations, tile_weights, biases, source_codes, send_list):
    row_count = activations.shape[0]
    tile_width = tile_weights.shape[3]
    block_count = source_codes.shape[1]
    fan_tiles = source_codes.shape[2]
    layer_count = tile_weights.shape[0]
    part_count = lax.axis_size("dom")
    own_index = lax.axis_index("dom")
    neighbor_offsets = (1, 2, -1, part_count // 2)
    offset_table = jnp.array(neighbor_offsets, jnp.int32)
    senders = (own_index - offset_table) % part_count
    destinations = (own_index + offset_table) % part_count
    current = activations.reshape(row_count, block_count, tile_width)
    for layer_index in range(layer_count):
        outgoing = jnp.take(current, send_list[layer_index, 0], axis=1)
        one_hot = (jnp.arange(part_count)[:, None] == destinations[None, :]).astype(jnp.bfloat16)
        out_blocks = jnp.einsum(
            "qn,rnc->qrc", one_hot, outgoing, preferred_element_type=jnp.float32
        ).astype(jnp.bfloat16)
        in_blocks = lax.all_to_all(out_blocks, "dom", split_axis=0, concat_axis=0, tiled=True)
        arrived = jnp.transpose(jnp.take(in_blocks, senders, axis=0), (1, 0, 2))
        block_pool = jnp.concatenate([current, arrived], axis=1)
        input_panel = jnp.take(block_pool, source_codes[layer_index].reshape(-1), axis=1)
        input_panel = input_panel.reshape(row_count, block_count, fan_tiles * tile_width)
        layer_bias = biases[layer_index].reshape(block_count, tile_width)
        summed = jnp.einsum(
            "rjc,jco->rjo",
            input_panel,
            lax.all_gather(tile_weights[layer_index], "batch", axis=1, tiled=True),
            preferred_element_type=jnp.float32,
        )
        current = jnp.maximum(summed + layer_bias[None], 0.0).astype(jnp.bfloat16)
    return current.reshape(row_count, block_count * tile_width)


def solution(mesh):
    in_specs = (
        P("batch", "dom"),
        P(None, "dom", "batch", None),
        P(None, "dom"),
        P(None, "dom", None),
        P(None, "dom", None),
    )
    out_specs = P("batch", "dom")
    return jax.shard_map(body, mesh=mesh, in_specs=in_specs, out_specs=out_specs, check_vma=False)
```

profile of v0, /device:TPU:10, one launch (start us, length us, event | category | flops | bytes accessed | tf_op | source)
XLA Modules:
  0.0 336.6 jit_solution(4580243394682207343)
XLA Ops:
  6.5 0.7 compare_and_fusion.1
  7.3 1.5 copy.71
  8.8 0.7 copy.75
  9.4 0.6 gather_fusion
  10.0 0.1 select_bitcast_fusion.11
  10.2 0.8 convolution_convert_fusion.3
  11.0 2.1 copy.74
  13.1 11.9 %all-to-all-start = ((bf16[32,256,128]{2,1,0:T(8,128)(2,1)}), bf16[32,256,128]{2,1,0:T(8,128)(2,1)}, u32[]{:S(2)}, u32[]{:S(2)}) async-start(bf16[32,256,128]{2,1,0:T(8,128)(2,1)} %copy.74), calls=%async_computation | async-start | bytes 4194304 | tf_op jit(solution)/shard_map/all_to_all | solution.py:26
  25.1 1.0 fusion.39
  26.5 47.8 %all-to-all-done = bf16[32,256,128]{2,1,0:T(8,128)(2,1)} async-done(((bf16[32,256,128]{2,1,0:T(8,128)(2,1)}), bf16[32,256,128]{2,1,0:T(8,128)(2,1)}, u32[]{:S(2)}, u32[]{:S(2)}) %all-to-all-start) | async-done | bytes 2097184 | tf_op jit(solution)/shard_map/all_to_all | solution.py:26
  74.3 2.2 gather_fusion.1
  76.5 0.1 select_bitcast_fusion.10
  76.6 0.1 pad_maximum_fusion
  76.7 3.1 gather_fusion.2
  79.8 4.6 %select_bitcast_fusion.3 = bf16[256,64,128]{2,0,1:T(8,128)(2,1)} fusion(bf16[64,256,128]{2,1,0:T(8,128)(2,1)} %gather_fusion.2, pred[64]{0:T(512)(128)(4,1)S(1)} %compare_and_fusion.6), kind=kLoop, calls=%fused_computation.15 | loop fusion | flops 2097152 | bytes 8388672 | tf_op jit(solution)/shard_map/jit(_take)/select_n | solution.py:29
  84.5 6.4 %copy.76 = bf16[256,64,128]{0,2,1:T(8,128)(2,1)} copy(bf16[256,64,128]{2,0,1:T(8,128)(2,1)} %select_bitcast_fusion.3) | data formatting | bytes 8388608 | tf_op jit(solution)/shard_map/jit(_take)/select_n | solution.py:29
  90.8 4.2 %fusion.16 = bf16[256,16,128]{2,0,1:T(8,128)(2,1)S(1)} fusion(bf16[256,16,512]{0,2,1:T(8,128)(2,1)} %bitcast.92, bf16[1,16,512,128]{3,2,1,0:T(8,128)(2,1)} %all-gather.9.cloned.1.call-done, f32[16,128]{1,0:T(8,128)S(1)} %bitcast.101), kind=kOutput, calls=%fused_computation.32 | convolution fusion | flops 538443776 | bytes 7348224 | tf_op jit(solution)/shard_map/rjc,jco->rjo/dot_general | solution.py:32
  95.1 0.6 gather_fusion.3
  95.7 0.1 select_bitcast_fusion.9
  95.8 0.8 convolution_convert_fusion.2
  96.6 2.2 copy.79
  98.8 6.9 %all-to-all-start.1 = ((bf16[32,256,128]{2,1,0:T(8,128)(2,1)}), bf16[32,256,128]{2,1,0:T(8,128)(2,1)S(1)}, u32[]{:S(2)}, u32[]{:S(2)}) async-start(bf16[32,256,128]{2,1,0:T(8,128)(2,1)} %copy.79), calls=%async_computation.1 | async-start | bytes 4194304 | tf_op jit(solution)/shard_map/all_to_all | solution.py:26
  105.7 0.2 all-gather.11.cloned.1.call-start
  105.9 0.5 all-gather.11.cloned.1.call-update
  106.7 47.6 %all-to-all-done.1 = bf16[32,256,128]{2,1,0:T(8,128)(2,1)S(1)} async-done(((bf16[32,256,128]{2,1,0:T(8,128)(2,1)}), bf16[32,256,128]{2,1,0:T(8,128)(2,1)S(1)}, u32[]{:S(2)}, u32[]{:S(2)}) %all-to-all-start.1) | async-done | bytes 2097184 | tf_op jit(solution)/shard_map/all_to_all | solution.py:26
  154.2 0.6 gather_fusion.4
  154.8 0.1 select_bitcast_fusion.8
  154.9 0.1 pad_maximum_fusion.1
  155.1 3.1 gather_fusion.5
  158.2 4.6 %select_bitcast_fusion.2 = bf16[256,64,128]{2,0,1:T(8,128)(2,1)} fusion(bf16[64,256,128]{2,1,0:T(8,128)(2,1)} %gather_fusion.5, pred[64]{0:T(512)(128)(4,1)S(1)} %compare_and_fusion.4), kind=kLoop, calls=%fused_computation.14 | loop fusion | flops 2097152 | bytes 8388672 | tf_op jit(solution)/shard_map/jit(_take)/select_n | solution.py:29
  162.8 6.4 %copy.80 = bf16[256,64,128]{0,2,1:T(8,128)(2,1)} copy(bf16[256,64,128]{2,0,1:T(8,128)(2,1)} %select_bitcast_fusion.2) | data formatting | bytes 8388608 | tf_op jit(solution)/shard_map/jit(_take)/select_n | solution.py:29
  169.2 4.2 %fusion.19 = bf16[256,16,128]{2,0,1:T(8,128)(2,1)S(1)} fusion(bf16[256,16,512]{0,2,1:T(8,128)(2,1)} %bitcast.93, bf16[1,16,512,128]{3,2,1,0:T(8,128)(2,1)} %all-gather.11.cloned.1.call-done, f32[16,128]{1,0:T(8,128)S(1)} %bitcast.100), kind=kOutput, calls=%fused_computation.33 | convolution fusion | flops 538443776 | bytes 7348224 | tf_op jit(solution)/shard_map/rjc,jco->rjo/dot_general | solution.py:32
  173.4 0.6 gather_fusion.6
  174.0 0.1 select_bitcast_fusion.7
  174.1 0.8 convolution_convert_fusion.1
  175.0 2.2 copy.83
  177.1 6.6 %all-to-all-start.2 = ((bf16[32,256,128]{2,1,0:T(8,128)(2,1)}), bf16[32,256,128]{2,1,0:T(8,128)(2,1)S(1)}, u32[]{:S(2)}, u32[]{:S(2)}) async-start(bf16[32,256,128]{2,1,0:T(8,128)(2,1)} %copy.83), calls=%async_computation.2 | async-start | bytes 4194304 | tf_op jit(solution)/shard_map/all_to_all | solution.py:26
  183.8 0.7 all-gather.13.cloned.1.call-update
  184.7 48.1 %all-to-all-done.2 = bf16[32,256,128]{2,1,0:T(8,128)(2,1)S(1)} async-done(((bf16[32,256,128]{2,1,0:T(8,128)(2,1)}), bf16[32,256,128]{2,1,0:T(8,128)(2,1)S(1)}, u32[]{:S(2)}, u32[]{:S(2)}) %all-to-all-start.2) | async-done | bytes 2097184 | tf_op jit(solution)/shard_map/all_to_all | solution.py:26
  232.8 0.6 gather_fusion.7
  233.5 0.1 pad_maximum_fusion.2
  233.6 3.1 gather_fusion.8
  236.7 4.6 %select_bitcast_fusion.1 = bf16[256,64,128]{2,0,1:T(8,128)(2,1)} fusion(bf16[64,256,128]{2,1,0:T(8,128)(2,1)} %gather_fusion.8, pred[64]{0:T(512)(128)(4,1)S(1)} %compare_and_fusion.2), kind=kLoop, calls=%fused_computation.13 | loop fusion | flops 2097152 | bytes 8388672 | tf_op jit(solution)/shard_map/jit(_take)/select_n | solution.py:29
  241.3 6.4 %copy.84 = bf16[256,64,128]{0,2,1:T(8,128)(2,1)} copy(bf16[256,64,128]{2,0,1:T(8,128)(2,1)} %select_bitcast_fusion.1) | data formatting | bytes 8388608 | tf_op jit(solution)/shard_map/jit(_take)/select_n | solution.py:29
  247.7 4.2 %fusion.22 = bf16[256,16,128]{2,0,1:T(8,128)(2,1)S(1)} fusion(bf16[256,16,512]{0,2,1:T(8,128)(2,1)} %bitcast.94, bf16[1,16,512,128]{3,2,1,0:T(8,128)(2,1)} %all-gather.13.cloned.1.call-done, f32[16,128]{1,0:T(8,128)S(1)} %bitcast.99), kind=kOutput, calls=%fused_computation.34 | convolution fusion | flops 538443776 | bytes 7348224 | tf_op jit(solution)/shard_map/rjc,jco->rjo/dot_general | solution.py:32
  251.9 0.6 gather_fusion.9
  252.5 0.1 select_bitcast_fusion.5
  252.6 0.8 convolution_convert_fusion
  253.5 2.2 copy.87
  255.6 5.7 %all-to-all-start.3 = ((bf16[32,256,128]{2,1,0:T(8,128)(2,1)}), bf16[32,256,128]{2,1,0:T(8,128)(2,1)S(1)}, u32[]{:S(2)}, u32[]{:S(2)}) async-start(bf16[32,256,128]{2,1,0:T(8,128)(2,1)} %copy.87), calls=%async_computation.3 | async-start | bytes 4194304 | tf_op jit(solution)/shard_map/all_to_all | solution.py:26
  261.4 0.3 all-gather.15.cloned.1.call-start
  261.6 0.9 copy.100
  262.8 28.3 %all-gather.15.cloned.1.call-done = bf16[1,16,512,128]{3,1,0,2:T(8,128)(2,1)} async-done(((bf16[1,16,64,128]{3,1,0,2:T(8,128)(2,1)}), bf16[1,16,512,128]{3,1,0,2:T(8,128)(2,1)}) %all-gather.15.cloned.1.call-update) | async-done | bytes 2097168 | tf_op jit(solution)/shard_map/all_gather | solution.py:35
  291.0 4.4 %copy.90 = bf16[1,16,512,128]{2,3,1,0:T(8,128)(2,1)} copy(bf16[1,16,512,128]{3,1,0,2:T(8,128)(2,1)} %all-gather.15.cloned.1.call-done) | data formatting | bytes 4194304 | tf_op jit(solution)/shard_map/all_gather | solution.py:35
  295.4 14.1 %all-to-all-done.3 = bf16[32,256,128]{2,1,0:T(8,128)(2,1)S(1)} async-done(((bf16[32,256,128]{2,1,0:T(8,128)(2,1)}), bf16[32,256,128]{2,1,0:T(8,128)(2,1)S(1)}, u32[]{:S(2)}, u32[]{:S(2)}) %all-to-all-start.3) | async-done | bytes 2097184 | tf_op jit(solution)/shard_map/all_to_all | solution.py:26
  309.4 0.6 gather_fusion.10
  310.0 0.1 select_bitcast_fusion.4
  310.1 0.1 pad_maximum_fusion.3
  310.3 3.1 gather_fusion.11
  313.4 4.6 %select_bitcast_fusion = bf16[256,64,128]{2,0,1:T(8,128)(2,1)} fusion(bf16[64,256,128]{2,1,0:T(8,128)(2,1)} %gather_fusion.11, pred[64]{0:T(512)(128)(4,1)S(1)} %compare_and_fusion), kind=kLoop, calls=%fused_computation.12 | loop fusion | flops 2097152 | bytes 8388672 | tf_op jit(solution)/shard_map/jit(_take)/select_n | solution.py:29
  318.0 6.5 %copy.88 = bf16[256,64,128]{0,2,1:T(8,128)(2,1)} copy(bf16[256,64,128]{2,0,1:T(8,128)(2,1)} %select_bitcast_fusion) | data formatting | bytes 8388608 | tf_op jit(solution)/shard_map/jit(_take)/select_n | solution.py:29
  324.5 3.6 %fusion.25 = bf16[256,16,128]{2,0,1:T(8,128)(2,1)S(1)} fusion(bf16[256,16,512]{0,2,1:T(8,128)(2,1)} %bitcast.95, bf16[1,16,512,128]{2,3,1,0:T(8,128)(2,1)S(1)} %copy-done, f32[16,128]{1,0:T(8,128)S(1)} %bitcast.98), kind=kOutput, calls=%fused_computation.35 | convolution fusion | flops 538443776 | bytes 7348224 | tf_op jit(solution)/shard_map/rjc,jco->rjo/dot_general | solution.py:32
  328.1 0.5 copy.93
  328.6 1.4 copy.94
  (51 shorter events, 1.1 us)
Async XLA Ops:
  8.8 1.4 copy-start.6
  13.1 12.0 %copy-start.1 = (bf16[4,16,64,128]{3,2,1,0:T(8,128)(2,1)S(1)}, bf16[4,16,64,128]{3,2,1,0:T(8,128)(2,1)}, u32[]{:S(2)}) copy-start(bf16[4,16,64,128]{3,2,1,0:T(8,128)(2,1)} %param.13) | copy-start | bytes 3145732
  13.1 61.2 %all-to-all-start = ((bf16[32,256,128]{2,1,0:T(8,128)(2,1)}), bf16[32,256,128]{2,1,0:T(8,128)(2,1)}, u32[]{:S(2)}, u32[]{:S(2)}) async-start(bf16[32,256,128]{2,1,0:T(8,128)(2,1)} %copy.74), calls=%async_computation | async-start | bytes 4194304 | tf_op jit(solution)/shard_map/all_to_all | solution.py:26
  25.0 1.1 copy-start.4
  25.0 1.3 copy-start.5
  25.1 1.4 copy-start.3
  25.1 65.8 %all-gather.9.cloned.1.call-start = ((), (), s32[]{:S(2)}) async-start(), calls=%async_computation.4 | async-start | bytes 2359296 | tf_op jit(solution)/shard_map/all_gather | solution.py:35
  98.8 55.4 %all-to-all-start.1 = ((bf16[32,256,128]{2,1,0:T(8,128)(2,1)}), bf16[32,256,128]{2,1,0:T(8,128)(2,1)S(1)}, u32[]{:S(2)}, u32[]{:S(2)}) async-start(bf16[32,256,128]{2,1,0:T(8,128)(2,1)} %copy.79), calls=%async_computation.1 | async-start | bytes 4194304 | tf_op jit(solution)/shard_map/all_to_all | solution.py:26
  105.7 63.5 %all-gather.11.cloned.1.call-start = ((), (), s32[]{:S(2)}) async-start(), calls=%async_computation.5 | async-start | bytes 2359296 | tf_op jit(solution)/shard_map/all_gather | solution.py:35
  177.1 55.6 %all-to-all-start.2 = ((bf16[32,256,128]{2,1,0:T(8,128)(2,1)}), bf16[32,256,128]{2,1,0:T(8,128)(2,1)S(1)}, u32[]{:S(2)}, u32[]{:S(2)}) async-start(bf16[32,256,128]{2,1,0:T(8,128)(2,1)} %copy.83), calls=%async_computation.2 | async-start | bytes 4194304 | tf_op jit(solution)/shard_map/all_to_all | solution.py:26
  183.7 64.0 %all-gather.13.cloned.1.call-start = ((), (), s32[]{:S(2)}) async-start(), calls=%async_computation.6 | async-start | bytes 2359296 | tf_op jit(solution)/shard_map/all_gather | solution.py:35
  255.6 6.0 %copy-start.2 = (bf16[1,16,64,128]{3,2,1,0:T(8,128)(2,1)S(1)}, bf16[1,16,64,128]{3,2,1,0:T(8,128)(2,1)}, u32[]{:S(2)}) copy-start(bf16[1,16,64,128]{3,2,1,0:T(8,128)(2,1)} %get-tuple-element.18) | copy-start | bytes 786436
  255.6 53.8 %all-to-all-start.3 = ((bf16[32,256,128]{2,1,0:T(8,128)(2,1)}), bf16[32,256,128]{2,1,0:T(8,128)(2,1)S(1)}, u32[]{:S(2)}, u32[]{:S(2)}) async-start(bf16[32,256,128]{2,1,0:T(8,128)(2,1)} %copy.87), calls=%async_computation.3 | async-start | bytes 4194304 | tf_op jit(solution)/shard_map/all_to_all | solution.py:26
  261.4 29.7 %all-gather.15.cloned.1.call-start = ((), (), s32[]{:S(2)}) async-start(), calls=%async_computation.7 | async-start | bytes 2359296 | tf_op jit(solution)/shard_map/all_gather | solution.py:35
  318.0 6.5 %copy-start = (bf16[1,16,512,128]{2,3,1,0:T(8,128)(2,1)S(1)}, bf16[1,16,512,128]{2,3,1,0:T(8,128)(2,1)}, u32[]{:S(2)}) copy-start(bf16[1,16,512,128]{2,3,1,0:T(8,128)(2,1)} %copy.90) | copy-start | bytes 6291460
Sparse Core Ops, SparseCore 0:
  27.7 27.2 all-gather.8
  108.3 27.4 all-gather.10
  186.4 27.2 all-gather.12
  263.7 27.2 all-gather.14
where the time goes:
time: 338 us; the launch traced here: 337 us
  waiting for transfers between devices  187 us (55%)
  local copies, waits for them, and re-layouts  64 us (19%)
  starting transfers between devices  31.6 us (9%)
  other arithmetic  20.6 us (6%)
  matrix products  19.6 us (6%)
  between operations  13.6 us (4%)
    all_to_all x4, waiting for transfers between devices, body(): lax.all_to_all(out_blocks, 'dom', split_axis=0, concat_axis=0, tiled=True)  158 us
    all_to_all x4, starting transfers between devices, body(): lax.all_to_all(out_blocks, 'dom', split_axis=0, concat_axis=0, tiled=True)  31 us
    all_gather x4, waiting for transfers between devices, body(): lax.all_gather(tile_weights[layer_index], 'batch', axis=1, tiled=True)  28.3 us
    select_n x4, local copies, waits for them, and re-layouts, body(): jnp.take(block_pool, source_codes[layer_index].reshape(-1), axis=1)  25.6 us
    select_n x8, other arithmetic, body(): jnp.take(block_pool, source_codes[layer_index].reshape(-1), axis=1)  18.6 us
    dot_general x4, matrix products, body(): jnp.einsum('rjc,jco->rjo', input_panel, lax.all_gather(tile_weights[layer...  16.3 us
    gather x4, local copies, waits for them, and re-layouts, body(): jnp.take(block_pool, source_codes[layer_index].reshape(-1), axis=1)  12.4 us
    convert_element_type x4, local copies, waits for them, and re-layouts, body(): out_blocks = jnp.einsum('qn,rnc->qrc', one_hot, outgoing, preferred_eleme...  8.6 us
  transfers between devices with their start and end apart: 8, of which 5 were waited for; matrix products, arithmetic and copies ran while one was open for 16% of the time, Pallas kernels for 0%

commit v1 on v0

--- a/solution.py
+++ b/solution.py
@@ -32,7 +32,12 @@
         summed = jnp.einsum(
             "rjc,jco->rjo",
             input_panel,
-            lax.all_gather(tile_weights[layer_index], "batch", axis=1, tiled=True),
+            jnp.concatenate(
+                lax.all_to_all(
+                    jnp.stack([tile_weights[layer_index]] * lax.axis_size("batch")), "batch", 0, 0
+                ),
+                axis=1,
+            ),
             preferred_element_type=jnp.float32,
         )
         current = jnp.maximum(summed + layer_bias[None], 0.0).astype(jnp.bfloat16)

time: 338 us -> 391 us (1.16)
  waiting for transfers between devices: 187 us -> 213 us
  starting transfers between devices: 31.6 us -> 52 us
  local copies, waits for them, and re-layouts: 64 us -> 82.2 us
  between operations: 13.6 us -> 0.44 us
    all_to_all x4, waiting for transfers between devices: 158 us -> 193 us  [body(): lax.all_to_all(out_blocks, 'dom', split_axis=0, concat_axis=0, tiled=True)]
    all_gather x4 -> x0, waiting for transfers between devices: 28.3 us -> none  [body(): lax.all_gather(tile_weights[layer_index], 'batch', axis=1, tiled=True)]
    all_to_all x0 -> x4, starting transfers between devices: none -> 20.3 us  [body(): lax.all_to_all(jnp.stack([tile_weights[layer_index]] * lax.axis_size('bat...]
    all_to_all x0 -> x4, waiting for transfers between devices: none -> 19.3 us  [body(): lax.all_to_all(jnp.stack([tile_weights[layer_index]] * lax.axis_size('bat...]
    another operation x0 -> x4, local copies, waits for them, and re-layouts: none -> 7.65 us  [body(): jnp.stack([tile_weights[layer_index]] * lax.axis_size('batch'))]
    reshape x0 -> x3, local copies, waits for them, and re-layouts: none -> 6.25 us  [body(): jnp.concatenate(lax.all_to_all(jnp.stack([tile_weights[layer_index]] * la...]
    all_gather x1 -> x0, local copies, waits for them, and re-layouts: 4.38 us -> none  [body(): lax.all_gather(tile_weights[layer_index], 'batch', axis=1, tiled=True)]
  transfers between devices with their start and end apart: 8 -> 8, of which waited for: 5 -> 6; matrix products, arithmetic and copies ran while one was open for 16% -> 24% of each run, Pallas kernels for 0% -> 0%
where the time goes in v1:
time: 391 us; the launch traced here: 389 us
  waiting for transfers between devices  213 us (54%)
  local copies, waits for them, and re-layouts  82.2 us (21%)
  starting transfers between devices  52 us (13%)
  other arithmetic  23.3 us (6%)
  matrix products  18.3 us (5%)
    all_to_all x4, waiting for transfers between devices, body(): lax.all_to_all(out_blocks, 'dom', split_axis=0, concat_axis=0, tiled=True)  193 us
    all_to_all x4, starting transfers between devices, body(): lax.all_to_all(out_blocks, 'dom', split_axis=0, concat_axis=0, tiled=True)  31.7 us
    select_n x4, local copies, waits for them, and re-layouts, body(): jnp.take(block_pool, source_codes[layer_index].reshape(-1), axis=1)  26 us
    all_to_all x4, starting transfers between devices, body(): lax.all_to_all(jnp.stack([tile_weights[layer_index]] * lax.axis_size('bat...  20.3 us
    all_to_all x4, waiting for transfers between devices, body(): lax.all_to_all(jnp.stack([tile_weights[layer_index]] * lax.axis_size('bat...  19.3 us
    select_n x8, other arithmetic, body(): jnp.take(block_pool, source_codes[layer_index].reshape(-1), axis=1)  18.6 us
    dot_general x4, matrix products, body(): jnp.einsum('rjc,jco->rjo', input_panel, jnp.concatenate(lax.all_to_all(jn...  14.9 us
    gather x4, local copies, waits for them, and re-layouts, body(): jnp.take(block_pool, source_codes[layer_index].reshape(-1), axis=1)  12.4 us
  transfers between devices with their start and end apart: 8, of which 6 were waited for; matrix products, arithmetic and copies ran while one was open for 24% of the time, Pallas kernels for 0%

profile of v1, /device:TPU:10, one launch (start us, length us, event | category | flops | bytes accessed | tf_op | source)
XLA Modules:
  0.0 388.8 jit_solution(12074115498981246567)
XLA Ops:
  0.0 2.1 slice_bitcast_fusion
  2.1 1.9 stack.12
  4.0 5.0 %all-to-all-start.1 = ((bf16[8,16,64,128]{3,2,1,0:T(8,128)(2,1)}), bf16[8,16,64,128]{3,2,1,0:T(8,128)(2,1)S(1)}, u32[]{:S(2)}, u32[]{:S(2)}) async-start(bf16[8,16,64,128]{3,2,1,0:T(8,128)(2,1)} %stack.12), calls=%async_computation.1 | async-start | bytes 4194304 | tf_op jit(solution)/shard_map/all_to_all | solution.py:36
  9.0 1.3 copy.71
  10.3 1.6 copy.75
  12.0 0.6 gather_fusion
  12.7 0.8 convolution_convert_fusion.3
  13.5 2.1 copy.74
  15.7 19.0 %all-to-all-done.1 = bf16[8,16,64,128]{3,2,1,0:T(8,128)(2,1)S(1)} async-done(((bf16[8,16,64,128]{3,2,1,0:T(8,128)(2,1)}), bf16[8,16,64,128]{3,2,1,0:T(8,128)(2,1)S(1)}, u32[]{:S(2)}, u32[]{:S(2)}) %all-to-all-start.1) | async-done | bytes 2097184 | tf_op jit(solution)/shard_map/all_to_all | solution.py:36
  34.7 11.8 %all-to-all-start = ((bf16[32,256,128]{2,1,0:T(8,128)(2,1)}), bf16[32,256,128]{2,1,0:T(8,128)(2,1)}, u32[]{:S(2)}, u32[]{:S(2)}) async-start(bf16[32,256,128]{2,1,0:T(8,128)(2,1)} %copy.74), calls=%async_computation | async-start | bytes 4194304 | tf_op jit(solution)/shard_map/all_to_all | solution.py:26
  46.8 48.7 %all-to-all-done = bf16[32,256,128]{2,1,0:T(8,128)(2,1)} async-done(((bf16[32,256,128]{2,1,0:T(8,128)(2,1)}), bf16[32,256,128]{2,1,0:T(8,128)(2,1)}, u32[]{:S(2)}, u32[]{:S(2)}) %all-to-all-start) | async-done | bytes 2097184 | tf_op jit(solution)/shard_map/all_to_all | solution.py:26
  95.4 1.9 stack.13
  97.3 5.7 %all-to-all-start.3 = ((bf16[8,16,64,128]{3,2,1,0:T(8,128)(2,1)}), bf16[8,16,64,128]{3,2,1,0:T(8,128)(2,1)}, u32[]{:S(2)}, u32[]{:S(2)}) async-start(bf16[8,16,64,128]{3,2,1,0:T(8,128)(2,1)} %stack.13), calls=%async_computation.3 | async-start | bytes 4194304 | tf_op jit(solution)/shard_map/all_to_all | solution.py:36
  103.0 1.6 copy.77
  104.6 2.2 gather_fusion.1
  106.9 0.1 pad_maximum_fusion
  107.0 3.1 gather_fusion.2
  110.1 4.6 %select_bitcast_fusion.3 = bf16[256,64,128]{2,0,1:T(8,128)(2,1)} fusion(bf16[64,256,128]{2,1,0:T(8,128)(2,1)} %gather_fusion.2, pred[64]{0:T(512)(128)(4,1)S(1)} %compare_and_fusion.6), kind=kLoop, calls=%fused_computation.15 | loop fusion | flops 2097152 | bytes 8388672 | tf_op jit(solution)/shard_map/jit(_take)/select_n | solution.py:29
  114.8 6.5 %copy.76 = bf16[256,64,128]{0,2,1:T(8,128)(2,1)} copy(bf16[256,64,128]{2,0,1:T(8,128)(2,1)} %select_bitcast_fusion.3) | data formatting | bytes 8388608 | tf_op jit(solution)/shard_map/jit(_take)/select_n | solution.py:29
  121.3 3.6 fusion
  124.9 0.6 gather_fusion.3
  125.6 0.8 convolution_convert_fusion.2
  126.4 2.2 copy.80
  128.6 0.3 all-to-all-done.3
  128.9 6.9 %all-to-all-start.2 = ((bf16[32,256,128]{2,1,0:T(8,128)(2,1)}), bf16[32,256,128]{2,1,0:T(8,128)(2,1)S(1)}, u32[]{:S(2)}, u32[]{:S(2)}) async-start(bf16[32,256,128]{2,1,0:T(8,128)(2,1)} %copy.80), calls=%async_computation.2 | async-start | bytes 4194304 | tf_op jit(solution)/shard_map/all_to_all | solution.py:26
  136.0 49.2 %all-to-all-done.2 = bf16[32,256,128]{2,1,0:T(8,128)(2,1)S(1)} async-done(((bf16[32,256,128]{2,1,0:T(8,128)(2,1)}), bf16[32,256,128]{2,1,0:T(8,128)(2,1)S(1)}, u32[]{:S(2)}, u32[]{:S(2)}) %all-to-all-start.2) | async-done | bytes 2097184 | tf_op jit(solution)/shard_map/all_to_all | solution.py:26
  185.2 2.0 stack.14
  187.2 4.8 %all-to-all-start.5 = ((bf16[8,16,64,128]{3,2,1,0:T(8,128)(2,1)}), bf16[8,16,64,128]{3,2,1,0:T(8,128)(2,1)S(1)}, u32[]{:S(2)}, u32[]{:S(2)}) async-start(bf16[8,16,64,128]{3,2,1,0:T(8,128)(2,1)} %stack.14), calls=%async_computation.5 | async-start | bytes 4194304 | tf_op jit(solution)/shard_map/all_to_all | solution.py:36
  192.0 3.1 copy.82
  195.1 2.2 gather_fusion.4
  197.4 1.3 pad_maximum_fusion.1
  198.8 3.1 gather_fusion.5
  201.9 4.6 %select_bitcast_fusion.2 = bf16[256,64,128]{2,0,1:T(8,128)(2,1)} fusion(bf16[64,256,128]{2,1,0:T(8,128)(2,1)} %gather_fusion.5, pred[64]{0:T(512)(128)(4,1)S(1)} %compare_and_fusion.4), kind=kLoop, calls=%fused_computation.14 | loop fusion | flops 2097152 | bytes 8388672 | tf_op jit(solution)/shard_map/jit(_take)/select_n | solution.py:29
  206.5 6.4 %copy.81 = bf16[256,64,128]{0,2,1:T(8,128)(2,1)} copy(bf16[256,64,128]{2,0,1:T(8,128)(2,1)} %select_bitcast_fusion.2) | data formatting | bytes 8388608 | tf_op jit(solution)/shard_map/jit(_take)/select_n | solution.py:29
  212.9 4.2 %fusion.1 = bf16[256,16,128]{2,0,1:T(8,128)(2,1)S(1)} fusion(bf16[256,16,512]{0,2,1:T(8,128)(2,1)} %bitcast.89, bf16[16,512,128]{2,1,0:T(8,128)(2,1)} %bitcast.95, f32[16,128]{1,0:T(8,128)S(1)} %bitcast.99), kind=kOutput, calls=%fused_computation.25 | convolution fusion | flops 538443776 | bytes 7348224 | tf_op jit(solution)/shard_map/rjc,jco->rjo/dot_general | solution.py:32
  217.2 1.3 gather_fusion.6
  218.5 1.0 select_bitcast_fusion.7
  219.5 0.8 convolution_convert_fusion.1
  220.4 2.1 copy.85
  222.5 6.8 %all-to-all-start.4 = ((bf16[32,256,128]{2,1,0:T(8,128)(2,1)}), bf16[32,256,128]{2,1,0:T(8,128)(2,1)}, u32[]{:S(2)}, u32[]{:S(2)}) async-start(bf16[32,256,128]{2,1,0:T(8,128)(2,1)} %copy.85), calls=%async_computation.4 | async-start | bytes 4194304 | tf_op jit(solution)/shard_map/all_to_all | solution.py:26
  229.5 49.4 %all-to-all-done.4 = bf16[32,256,128]{2,1,0:T(8,128)(2,1)} async-done(((bf16[32,256,128]{2,1,0:T(8,128)(2,1)}), bf16[32,256,128]{2,1,0:T(8,128)(2,1)}, u32[]{:S(2)}, u32[]{:S(2)}) %all-to-all-start.4) | async-done | bytes 2097184 | tf_op jit(solution)/shard_map/all_to_all | solution.py:26
  278.9 1.9 stack.15
  280.7 4.8 %all-to-all-start.7 = ((bf16[8,16,64,128]{3,2,1,0:T(8,128)(2,1)}), bf16[8,16,64,128]{3,2,1,0:T(8,128)(2,1)}, u32[]{:S(2)}, u32[]{:S(2)}) async-start(bf16[8,16,64,128]{3,2,1,0:T(8,128)(2,1)} %stack.15), calls=%async_computation.7 | async-start | bytes 4194304 | tf_op jit(solution)/shard_map/all_to_all | solution.py:36
  285.6 1.6 copy.87
  287.1 2.2 gather_fusion.7
  289.4 1.3 pad_maximum_fusion.2
  290.8 3.1 gather_fusion.8
  293.9 4.7 %select_bitcast_fusion.1 = bf16[256,64,128]{2,0,1:T(8,128)(2,1)} fusion(bf16[64,256,128]{2,1,0:T(8,128)(2,1)} %gather_fusion.8, pred[64]{0:T(512)(128)(4,1)S(1)} %compare_and_fusion.2), kind=kLoop, calls=%fused_computation.13 | loop fusion | flops 2097152 | bytes 8388672 | tf_op jit(solution)/shard_map/jit(_take)/select_n | solution.py:29
  298.5 6.5 %copy.86 = bf16[256,64,128]{0,2,1:T(8,128)(2,1)} copy(bf16[256,64,128]{2,0,1:T(8,128)(2,1)} %select_bitcast_fusion.1) | data formatting | bytes 8388608 | tf_op jit(solution)/shard_map/jit(_take)/select_n | solution.py:29
  305.1 3.6 fusion.2
  308.6 0.6 gather_fusion.9
  309.3 0.8 convolution_convert_fusion
  310.2 2.2 copy.90
  312.3 6.3 %all-to-all-start.6 = ((bf16[32,256,128]{2,1,0:T(8,128)(2,1)}), bf16[32,256,128]{2,1,0:T(8,128)(2,1)S(1)}, u32[]{:S(2)}, u32[]{:S(2)}) async-start(bf16[32,256,128]{2,1,0:T(8,128)(2,1)} %copy.90), calls=%async_computation.6 | async-start | bytes 4194304 | tf_op jit(solution)/shard_map/all_to_all | solution.py:26
  318.9 3.2 copy.92
  322.1 46.1 %all-to-all-done.6 = bf16[32,256,128]{2,1,0:T(8,128)(2,1)S(1)} async-done(((bf16[32,256,128]{2,1,0:T(8,128)(2,1)}), bf16[32,256,128]{2,1,0:T(8,128)(2,1)S(1)}, u32[]{:S(2)}, u32[]{:S(2)}) %all-to-all-start.6) | async-done | bytes 2097184 | tf_op jit(solution)/shard_map/all_to_all | solution.py:26
  368.2 0.6 gather_fusion.10
  368.9 0.1 pad_maximum_fusion.3
  369.0 3.1 gather_fusion.11
  372.1 4.6 %select_bitcast_fusion = bf16[256,64,128]{2,0,1:T(8,128)(2,1)} fusion(bf16[64,256,128]{2,1,0:T(8,128)(2,1)} %gather_fusion.11, pred[64]{0:T(512)(128)(4,1)S(1)} %compare_and_fusion), kind=kLoop, calls=%fused_computation.12 | loop fusion | flops 2097152 | bytes 8388672 | tf_op jit(solution)/shard_map/jit(_take)/select_n | solution.py:29
  376.7 6.5 %copy.91 = bf16[256,64,128]{0,2,1:T(8,128)(2,1)} copy(bf16[256,64,128]{2,0,1:T(8,128)(2,1)} %select_bitcast_fusion) | data formatting | bytes 8388608 | tf_op jit(solution)/shard_map/jit(_take)/select_n | solution.py:29
  383.3 3.6 fusion.3
  386.8 0.5 copy.96
  387.4 1.4 copy.97
  (67 shorter events, 1.6 us)
Async XLA Ops:
  4.0 5.0 %copy-start.6 = (bf16[256,2048]{1,0:T(8,128)(2,1)S(1)}, bf16[256,2048]{1,0:T(8,128)(2,1)}, u32[]{:S(2)}) copy-start(bf16[256,2048]{1,0:T(8,128)(2,1)} %param.12) | copy-start | bytes 3145732
  4.0 30.7 %all-to-all-start.1 = ((bf16[8,16,64,128]{3,2,1,0:T(8,128)(2,1)}), bf16[8,16,64,128]{3,2,1,0:T(8,128)(2,1)S(1)}, u32[]{:S(2)}, u32[]{:S(2)}) async-start(bf16[8,16,64,128]{3,2,1,0:T(8,128)(2,1)} %stack.12), calls=%async_computation.1 | async-start | bytes 4194304 | tf_op jit(solution)/shard_map/all_to_all | solution.py:36
  9.0 2.9 copy-start.12
  9.0 3.6 copy-start.14
  15.7 30.8 %copy-start.11 = (s32[4,16,4]{1,2,0:T(4,128)S(1)}, s32[4,16,4]{1,2,0:T(4,128)}, u32[]{:S(2)}) copy-start(s32[4,16,4]{1,2,0:T(4,128)} %param.15) | copy-start | bytes 3076
  15.7 31.0 %copy-start.13 = (s32[4]{0:T(128)S(1)}, s32[4]{0:T(128)}, u32[]{:S(2)}) copy-start(s32[4]{0:T(128)} %constant.64) | copy-start | bytes 52
  15.7 31.0 %copy-start.10 = (f32[4,2048]{1,0:T(4,128)S(1)}, f32[4,2048]{1,0:T(4,128)}, u32[]{:S(2)}) copy-start(f32[4,2048]{1,0:T(4,128)} %param.14) | copy-start | bytes 98308
  15.7 79.7 %copy-start.9 = (bf16[16,64,128]{2,1,0:T(8,128)(2,1)S(1)}, bf16[16,64,128]{2,1,0:T(8,128)(2,1)}, u32[]{:S(2)}) copy-start(bf16[16,64,128]{2,1,0:T(8,128)(2,1)} %get-tuple-element.19) | copy-start | bytes 786436
  34.7 60.8 %all-to-all-start = ((bf16[32,256,128]{2,1,0:T(8,128)(2,1)}), bf16[32,256,128]{2,1,0:T(8,128)(2,1)}, u32[]{:S(2)}, u32[]{:S(2)}) async-start(bf16[32,256,128]{2,1,0:T(8,128)(2,1)} %copy.74), calls=%async_computation | async-start | bytes 4194304 | tf_op jit(solution)/shard_map/all_to_all | solution.py:26
  97.3 31.6 %all-to-all-start.3 = ((bf16[8,16,64,128]{3,2,1,0:T(8,128)(2,1)}), bf16[8,16,64,128]{3,2,1,0:T(8,128)(2,1)}, u32[]{:S(2)}, u32[]{:S(2)}) async-start(bf16[8,16,64,128]{3,2,1,0:T(8,128)(2,1)} %stack.13), calls=%async_computation.3 | async-start | bytes 4194304 | tf_op jit(solution)/shard_map/all_to_all | solution.py:36
  114.8 6.5 %copy-start.2 = (bf16[16,8,64,128]{3,2,1,0:T(8,128)(2,1)S(1)}, bf16[16,8,64,128]{3,2,1,0:T(8,128)(2,1)}, u32[]{:S(2)}) copy-start(bf16[16,8,64,128]{3,2,1,0:T(8,128)(2,1)} %copy.77) | copy-start | bytes 6291460
  124.9 3.7 copy-start.4
  128.6 56.6 %copy-start.8 = (bf16[16,64,128]{2,1,0:T(8,128)(2,1)S(1)}, bf16[16,64,128]{2,1,0:T(8,128)(2,1)}, u32[]{:S(2)}) copy-start(bf16[16,64,128]{2,1,0:T(8,128)(2,1)} %get-tuple-element.21) | copy-start | bytes 786436
  128.9 56.3 %all-to-all-start.2 = ((bf16[32,256,128]{2,1,0:T(8,128)(2,1)}), bf16[32,256,128]{2,1,0:T(8,128)(2,1)S(1)}, u32[]{:S(2)}, u32[]{:S(2)}) async-start(bf16[32,256,128]{2,1,0:T(8,128)(2,1)} %copy.80), calls=%async_computation.2 | async-start | bytes 4194304 | tf_op jit(solution)/shard_map/all_to_all | solution.py:26
  185.1 2.0 copy-start
  187.2 35.4 %all-to-all-start.5 = ((bf16[8,16,64,128]{3,2,1,0:T(8,128)(2,1)}), bf16[8,16,64,128]{3,2,1,0:T(8,128)(2,1)S(1)}, u32[]{:S(2)}, u32[]{:S(2)}) async-start(bf16[8,16,64,128]{3,2,1,0:T(8,128)(2,1)} %stack.14), calls=%async_computation.5 | async-start | bytes 4194304 | tf_op jit(solution)/shard_map/all_to_all | solution.py:36
  217.2 5.4 %copy-start.5 = (bf16[256,16,128]{2,0,1:T(8,128)(2,1)}, bf16[256,16,128]{2,0,1:T(8,128)(2,1)S(1)}, u32[]{:S(2)}) copy-start(bf16[256,16,128]{2,0,1:T(8,128)(2,1)S(1)} %fusion.1) | copy-start | bytes 3145732
  222.5 56.3 %copy-start.7 = (bf16[16,64,128]{2,1,0:T(8,128)(2,1)S(1)}, bf16[16,64,128]{2,1,0:T(8,128)(2,1)}, u32[]{:S(2)}) copy-start(bf16[16,64,128]{2,1,0:T(8,128)(2,1)} %get-tuple-element.18) | copy-start | bytes 786436
  222.5 56.3 %all-to-all-start.4 = ((bf16[32,256,128]{2,1,0:T(8,128)(2,1)}), bf16[32,256,128]{2,1,0:T(8,128)(2,1)}, u32[]{:S(2)}, u32[]{:S(2)}) async-start(bf16[32,256,128]{2,1,0:T(8,128)(2,1)} %copy.85), calls=%async_computation.4 | async-start | bytes 4194304 | tf_op jit(solution)/shard_map/all_to_all | solution.py:26
  280.7 31.6 %all-to-all-start.7 = ((bf16[8,16,64,128]{3,2,1,0:T(8,128)(2,1)}), bf16[8,16,64,128]{3,2,1,0:T(8,128)(2,1)}, u32[]{:S(2)}, u32[]{:S(2)}) async-start(bf16[8,16,64,128]{3,2,1,0:T(8,128)(2,1)} %stack.15), calls=%async_computation.7 | async-start | bytes 4194304 | tf_op jit(solution)/shard_map/all_to_all | solution.py:36
  298.5 6.5 %copy-start.3 = (bf16[16,8,64,128]{3,2,1,0:T(8,128)(2,1)S(1)}, bf16[16,8,64,128]{3,2,1,0:T(8,128)(2,1)}, u32[]{:S(2)}) copy-start(bf16[16,8,64,128]{3,2,1,0:T(8,128)(2,1)} %copy.87) | copy-start | bytes 6291460
  312.3 55.8 %all-to-all-start.6 = ((bf16[32,256,128]{2,1,0:T(8,128)(2,1)}), bf16[32,256,128]{2,1,0:T(8,128)(2,1)S(1)}, u32[]{:S(2)}, u32[]{:S(2)}) async-start(bf16[32,256,128]{2,1,0:T(8,128)(2,1)} %copy.90), calls=%async_computation.6 | async-start | bytes 4194304 | tf_op jit(solution)/shard_map/all_to_all | solution.py:26
  376.7 6.5 %copy-start.1 = (bf16[8,16,64,128]{3,2,0,1:T(8,128)(2,1)S(1)}, bf16[8,16,64,128]{3,2,0,1:T(8,128)(2,1)}, u32[]{:S(2)}) copy-start(bf16[8,16,64,128]{3,2,0,1:T(8,128)(2,1)} %copy.92) | copy-start | bytes 6291460
